TPU v7x, 32 devices: a whole 2x2x4 slice. The times are simulated.
32 devices in a mesh: dp: 4 (over x, core), tensor: 8 (over z, y).
Axes of the slice: x: 2, y: 2, z: 4, core: 2. Of those that a mesh axis runs over, the one named last changes fastest.
Arguments:
- tokens: bfloat16 [2, 2048, 4, 1024], P(None, 'tensor', 'dp'), may hold values from -6 to 6
- cotangent: bfloat16 [2, 2048, 4, 1024], P(None, 'tensor', 'dp'), may hold values from -6 to 6
- timesteps: int32 [2, 4, 2], P(None, 'dp'), may hold values from 0 to 999
- bucket: int32 [2, 4], P(None, 'dp'), may hold values 0 or 1
- counts: int32 [2, 4], P(None, 'dp'), may hold values from 8 to 48, as said below
- qkv_weight: bfloat16 [3, 1024, 1024], P(None, None, 'tensor'), may hold values from -0.1875 to 0.1875
- qv_bias: float32 [2, 1024], P(None, 'tensor'), may hold values from -3 to 3
- out_weight: bfloat16 [1024, 1024], P('tensor'), may hold values from -2 to 2
- out_bias: float32 [1024], replicated, may hold values from -2 to 2
- norm1_gain: float32 [1024], replicated, may hold values from 0.25 to 1.75
- norm1_bias: float32 [1024], replicated, may hold values from -2 to 2
- up_weight: bfloat16 [1024, 4096], P(None, 'tensor'), may hold values from -0.1875 to 0.1875
- up_bias: float32 [4096], P('tensor'), may hold values from -3 to 3
- down_weight: bfloat16 [4096, 1024], P('tensor'), may hold values from -0.09375 to 0.09375
- down_bias: float32 [1024], replicated, may hold values from -2 to 2
- norm2_gain: float32 [1024], replicated, may hold values from 0.25 to 1.75
- norm2_bias: float32 [1024], replicated, may hold values from -2 to 2
Outputs:
- layer_out: bfloat16 [2, 2048, 4, 1024], P(None, 'tensor', 'dp')
- tokens_grad: float32 [2, 2048, 4, 1024], P(None, 'tensor', 'dp')
- qkv_grad: float32 [3, 1024, 1024], P(None, 'dp', 'tensor')
- qv_bias_grad: float32 [2, 1024], P(None, ('tensor', 'dp'))
- out_weight_grad: float32 [1024, 1024], P('tensor', 'dp')
- up_weight_grad: float32 [1024, 4096], P('dp', 'tensor')
- up_bias_grad: float32 [4096], P(('tensor', 'dp'))
- down_weight_grad: float32 [4096, 1024], P('tensor', 'dp')
- vector_grads: float32 [6, 1024], P(None, ('dp', 'tensor'))
Inputs may be any that keep to these rules, and one draw needn't show every extreme that they name: True counts are positive.
All inputs are finite; a program needn't handle non-finite values. No bound on the sum of `bucket` on one device may be relied on, other than what follows from the above.
Results may differ from a plain program's by a relative error of at most 0.02.
Values may be sent and summed in bfloat16 or wider, within the bound.
A program may use at most 320 MiB of HBM per device.

v0:
```python
import math
import jax
import jax.numpy as jnp
from jax import lax
from jax.sharding import PartitionSpec as P

HD = 64
EPS = 1e-05
INV_ROOT_TWO = 1.0 / math.sqrt(2.0)
INV_ROOT_TWO_PI = 1.0 / math.sqrt(2.0 * math.pi)


def as_sent(array):

    def short(part):
        return part.astype(jnp.bfloat16) if part.dtype == jnp.float32 else part

    return jax.tree.map(short, array)


def sinusoid(steps, width):
    half_width = width // 2
    freqs = jnp.exp(jnp.arange(half_width).astype(jnp.float32) * (-2.0 * math.log(10000.0) / width))
    angles = steps.astype(jnp.float32)[..., None] * freqs
    return jnp.concatenate([jnp.sin(angles), jnp.cos(angles)], axis=-1)


def norm_forward(values, gain, shift):
    average = jnp.mean(values, axis=-1, keepdims=True)
    centred = values - average
    spread = jnp.mean(centred * centred, axis=-1, keepdims=True)
    inverse = lax.rsqrt(spread + EPS)
    unit = centred * inverse
    return (unit * gain + shift, unit, inverse)


def norm_backward(grad, unit, inverse, gain):
    scaled = grad * gain
    first = jnp.mean(scaled, axis=-1, keepdims=True)
    second = jnp.mean(scaled * unit, axis=-1, keepdims=True)
    return inverse * (scaled - first - unit * second)


def gelu_slope(pre):
    return (
        0.5 * (1.0 + lax.erf(pre * INV_ROOT_TWO))
        + pre * jnp.exp(-0.5 * pre * pre) * INV_ROOT_TWO_PI
    )


def add_trees(left, right):
    if left is None:
        return right
    return jax.tree.map(lambda first_one, second_one: first_one + second_one, left, right)


def body(
    tokens,
    cotangent,
    timesteps,
    bucket,
    counts,
    qkv_weight,
    qv_bias,
    out_weight,
    out_bias,
    norm1_gain,
    norm1_bias,
    up_weight,
    up_bias,
    down_weight,
    down_bias,
    norm2_gain,
    norm2_bias,
):
    micro, segment, items_loc, width = tokens.shape
    parts = lax.axis_size("tensor")
    seq_len = segment * parts
    half_len = seq_len // 2
    columns = qkv_weight.shape[2]
    heads_loc = columns // HD
    scale = float(HD) ** (-0.5)
    position = lax.axis_index("tensor") * segment + jnp.arange(segment)
    late = position >= half_len
    count_f = counts.astype(jnp.float32)
    total = lax.psum(jnp.sum(count_f), "dp")
    items_all = micro * items_loc * lax.axis_size("dp")
    item_weight = count_f * float(items_all) / total
    outputs = []
    input_grads = []
    totals = None
    vector_total = jnp.zeros((6, width), jnp.float32)
    for index in range(micro):
        embedded = sinusoid(timesteps[index], width)
        temb = jnp.where(late[:, None, None], embedded[None, :, 1], embedded[None, :, 0])
        hidden = tokens[index].astype(jnp.float32) + temb
        hidden_low = hidden.astype(jnp.bfloat16)
        hidden_all = lax.all_gather(hidden_low, "tensor", axis=0, tiled=True)
        projected = jnp.einsum(
            "sid,kdc->ksic", hidden_all, qkv_weight, preferred_element_type=jnp.float32
        )
        q_heads = (
            (projected[0] + qv_bias[0])
            .astype(jnp.bfloat16)
            .reshape(seq_len, items_loc, heads_loc, HD)
        )
        k_heads = projected[1].astype(jnp.bfloat16).reshape(seq_len, items_loc, heads_loc, HD)
        v_heads = (
            (projected[2] + qv_bias[1])
            .astype(jnp.bfloat16)
            .reshape(seq_len, items_loc, heads_loc, HD)
        )
        logsums = []
        pieces = []
        for block in range(2):
            limit = (block + 1) * half_len
            scores = (
                jnp.einsum(
                    "qihd,kihd->ihqk",
                    q_heads[block * half_len : limit],
                    k_heads[:limit],
                    preferred_element_type=jnp.float32,
                )
                * scale
            )
            highest = jnp.max(scores, axis=-1, keepdims=True)
            logsum = highest + jnp.log(jnp.sum(jnp.exp(scores - highest), axis=-1, keepdims=True))
            probs_low = jnp.exp(scores - logsum).astype(jnp.bfloat16)
            pieces.append(
                jnp.einsum(
                    "ihqk,kihd->qihd",
                    probs_low,
                    v_heads[:limit],
                    preferred_element_type=jnp.float32,
                )
            )
            logsums.append(logsum)
        context = (
            jnp.concatenate(pieces, axis=0)
            .reshape(seq_len, items_loc, columns)
            .astype(jnp.bfloat16)
        )
        attention = lax.psum_scatter(
            jnp.einsum(
                "sic,cd->sid", context, out_weight, preferred_element_type=jnp.float32
            ).astype(jnp.bfloat16),
            "tensor",
            scatter_dimension=0,
            tiled=True,
        ).astype(jnp.float32)
        normed, unit_one, inverse_one = norm_forward(
            hidden + (attention + out_bias), norm1_gain, norm1_bias
        )
        normed_low = normed.astype(jnp.bfloat16)
        normed_all = lax.all_gather(normed_low, "tensor", axis=0, tiled=True)
        pre = (
            jnp.einsum("sid,df->sif", normed_all, up_weight, preferred_element_type=jnp.float32)
            + up_bias
        )
        act_low = jax.nn.gelu(pre, approximate=False).astype(jnp.bfloat16)
        branch = lax.psum_scatter(
            jnp.einsum(
                "sif,fd->sid", act_low, down_weight, preferred_element_type=jnp.float32
            ).astype(jnp.bfloat16),
            "tensor",
            scatter_dimension=0,
            tiled=True,
        ).astype(jnp.float32)
        result, unit_two, inverse_two = norm_forward(
            normed + (branch + down_bias), norm2_gain, norm2_bias
        )
        outputs.append(result.astype(jnp.bfloat16))
        keep = jnp.where(late[:, None], bucket[index][None, :], 1).astype(jnp.float32)
        grad_out = (
            cotangent[index].astype(jnp.float32)
            * item_weight[index][None, :, None]
            * keep[:, :, None]
        )
        gain_two_grad = jnp.sum(grad_out * unit_two, axis=(0, 1))
        shift_two_grad = jnp.sum(grad_out, axis=(0, 1))
        grad_sum = norm_backward(grad_out, unit_two, inverse_two, norm2_gain)
        down_bias_grad = jnp.sum(grad_sum, axis=(0, 1))
        grad_sum_all = lax.all_gather(grad_sum.astype(jnp.bfloat16), "tensor", axis=0, tiled=True)
        grad_act = jnp.einsum(
            "sid,fd->sif", grad_sum_all, down_weight, preferred_element_type=jnp.float32
        )
        down_grad = jnp.einsum(
            "sif,sid->fd", act_low, grad_sum_all, preferred_element_type=jnp.float32
        )
        grad_pre = (grad_act * gelu_slope(pre)).astype(jnp.bfloat16)
        up_bias_part = jnp.sum(grad_pre, axis=(0, 1), dtype=jnp.float32)
        up_grad = jnp.einsum(
            "sid,sif->df", normed_all, grad_pre, preferred_element_type=jnp.float32
        )
        grad_through = lax.psum_scatter(
            jnp.einsum(
                "sif,df->sid", grad_pre, up_weight, preferred_element_type=jnp.float32
            ).astype(jnp.bfloat16),
            "tensor",
            scatter_dimension=0,
            tiled=True,
        ).astype(jnp.float32)
        grad_normed = grad_sum + grad_through
        gain_one_grad = jnp.sum(grad_normed * unit_one, axis=(0, 1))
        shift_one_grad = jnp.sum(grad_normed, axis=(0, 1))
        grad_mixed = norm_backward(grad_normed, unit_one, inverse_one, norm1_gain)
        out_bias_grad = jnp.sum(grad_mixed, axis=(0, 1))
        grad_mixed_all = lax.all_gather(
            grad_mixed.astype(jnp.bfloat16), "tensor", axis=0, tiled=True
        )
        grad_context = jnp.einsum(
            "sid,cd->sic", grad_mixed_all, out_weight, preferred_element_type=jnp.float32
        ).astype(jnp.bfloat16)
        out_grad = jnp.einsum(
            "sic,sid->cd", context, grad_mixed_all, preferred_element_type=jnp.float32
        )
        grad_ctx_heads = grad_context.reshape(seq_len, items_loc, heads_loc, HD)
        query_grads = []
        key_total = jnp.zeros((seq_len, items_loc, heads_loc, HD), jnp.float32)
        value_total = jnp.zeros((seq_len, items_loc, heads_loc, HD), jnp.float32)
        for block in range(2):
            limit = (block + 1) * half_len
            rows_q = q_heads[block * half_len : limit]
            rows_grad = grad_ctx_heads[block * half_len : limit]
            scores = (
                jnp.einsum(
                    "qihd,kihd->ihqk", rows_q, k_heads[:limit], preferred_element_type=jnp.float32
                )
                * scale
            )
            probs = jnp.exp(scores - logsums[block])
            probs_low = probs.astype(jnp.bfloat16)
            grad_probs = jnp.einsum(
                "qihd,kihd->ihqk", rows_grad, v_heads[:limit], preferred_element_type=jnp.float32
            )
            value_part = jnp.einsum(
                "ihqk,qihd->kihd", probs_low, rows_grad, preferred_element_type=jnp.float32
            )
            grad_scores = (
                probs * (grad_probs - jnp.sum(probs * grad_probs, axis=-1, keepdims=True))
            ).astype(jnp.bfloat16)
            query_grads.append(
                jnp.einsum(
                    "ihqk,kihd->qihd",
                    grad_scores,
                    k_heads[:limit],
                    preferred_element_type=jnp.float32,
                )
                * scale
            )
            key_part = (
                jnp.einsum(
                    "ihqk,qihd->kihd", grad_scores, rows_q, preferred_element_type=jnp.float32
                )
                * scale
            )
            padding = ((0, seq_len - limit), (0, 0), (0, 0), (0, 0))
            key_total = key_total + jnp.pad(key_part, padding)
            value_total = value_total + jnp.pad(value_part, padding)
        grad_queries = (
            jnp.concatenate(query_grads, axis=0)
            .reshape(seq_len, items_loc, columns)
            .astype(jnp.bfloat16)
        )
        grad_keys = key_total.reshape(seq_len, items_loc, columns).astype(jnp.bfloat16)
        grad_values = value_total.reshape(seq_len, items_loc, columns).astype(jnp.bfloat16)
        grad_stack = jnp.stack([grad_queries, grad_keys, grad_values])
        bias_grad = jnp.stack(
            [
                jnp.sum(grad_queries, axis=(0, 1), dtype=jnp.float32),
                jnp.sum(grad_values, axis=(0, 1), dtype=jnp.float32),
            ]
        )
        qkv_part = jnp.einsum(
            "sid,ksic->kdc", hidden_all, grad_stack, preferred_element_type=jnp.float32
        )
        grad_proj = lax.psum_scatter(
            jnp.einsum(
                "ksic,kdc->sid", grad_stack, qkv_weight, preferred_element_type=jnp.float32
            ).astype(jnp.bfloat16),
            "tensor",
            scatter_dimension=0,
            tiled=True,
        ).astype(jnp.float32)
        grad_hidden = grad_mixed + grad_proj
        input_grads.append(grad_hidden)
        vector_total = vector_total + jnp.stack(
            [
                out_bias_grad,
                gain_one_grad,
                shift_one_grad,
                down_bias_grad,
                gain_two_grad,
                shift_two_grad,
            ]
        )
        micro_grads = (qkv_part, bias_grad, up_grad[None], up_bias_part[None], out_grad, down_grad)
        totals = add_trees(totals, micro_grads)
    totals = jax.tree.map(
        lambda part: part.astype(jnp.float32),
        lax.psum_scatter(as_sent(totals), "dp", scatter_dimension=1, tiled=True),
    )
    vector_grads = lax.psum_scatter(vector_total, ("dp", "tensor"), scatter_dimension=1, tiled=True)
    layer_out = jnp.stack(outputs)
    tokens_grad = jnp.stack(input_grads)
    return (
        layer_out,
        tokens_grad,
        totals[0],
        totals[1],
        totals[4],
        totals[2][0],
        totals[3][0],
        totals[5],
        vector_grads,
    )


def solution(mesh):
    placed = (
        P(None, "tensor", "dp", None),
        P(None, "tensor", "dp", None),
        P(None, "dp", None),
        P(None, "dp"),
        P(None, "dp"),
        P(None, None, "tensor"),
        P(None, "tensor"),
        P("tensor", None),
        P(),
        P(),
        P(),
        P(None, "tensor"),
        P("tensor"),
        P("tensor", None),
        P(),
        P(),
        P(),
    )
    return jax.shard_map(
        body,
        mesh=mesh,
        in_specs=placed,
        out_specs=(
            P(None, "tensor", "dp", None),
            P(None, "tensor", "dp", None),
            P(None, "dp", "tensor"),
            P(None, ("tensor", "dp")),
            P("tensor", "dp"),
            P("dp", "tensor"),
            P(("tensor", "dp")),
            P("tensor", "dp"),
            P(None, ("dp", "tensor")),
        ),
        check_vma=False,
    )
```

profile of v0, /device:TPU:0, one launch (start us, length us, event | category | flops | bytes accessed | tf_op | source)
XLA Modules:
  0.0 1731.8 jit_solution(11281601683911485581)
XLA Ops:
  13.5 72.8 %all-gather.9.cloned.1.call-done = bf16[2048,1,1024]{2,0,1:T(8,128)(2,1)} async-done(((bf16[256,1,1024]{2,0,1:T(8,128)(2,1)}), bf16[2048,1,1024]{2,0,1:T(8,128)(2,1)}) %all-gather.9.cloned.1.call-update) | async-done | bytes 4194320 | tf_op jit(solution)/shard_map/all_gather | solution.py:98
  111.0 86.9 %reduce-scatter.22.cloned.1.call-done = bf16[256,1,1024]{2,0,1:T(8,128)(2,1)} async-done(((bf16[2048,1,1024]{2,0,1:T(8,128)(2,1)}), bf16[256,1,1024]{2,0,1:T(8,128)(2,1)}) %reduce-scatter.22.cloned.1.call-update) | async-done | bytes 524304 | tf_op jit(solution)/shard_map/reduce_scatter | solution.py:143
  201.3 72.0 %all-gather.13.cloned.1.call-done = bf16[2048,1,1024]{2,0,1:T(8,128)(2,1)} async-done(((bf16[256,1,1024]{2,0,1:T(8,128)(2,1)}), bf16[2048,1,1024]{2,0,1:T(8,128)(2,1)}) %all-gather.13.cloned.1.call-update) | async-done | bytes 4194320 | tf_op jit(solution)/shard_map/all_gather | solution.py:98
  299.1 86.9 %reduce-scatter.26.cloned.1.call-done = bf16[256,1,1024]{2,0,1:T(8,128)(2,1)} async-done(((bf16[2048,1,1024]{2,0,1:T(8,128)(2,1)}), bf16[256,1,1024]{2,0,1:T(8,128)(2,1)}) %reduce-scatter.26.cloned.1.call-update) | async-done | bytes 524304 | tf_op jit(solution)/shard_map/reduce_scatter | solution.py:143
  389.1 72.5 %all-gather.11.cloned.1.call-done = bf16[2048,1,1024]{2,0,1:T(8,128)(2,1)} async-done(((bf16[256,1,1024]{2,0,1:T(8,128)(2,1)}), bf16[2048,1,1024]{2,0,1:T(8,128)(2,1)}) %all-gather.11.cloned.1.call-update) | async-done | bytes 4194320 | tf_op jit(solution)/shard_map/all_gather | solution.py:155
  461.7 14.0 fusion.6
  491.4 77.0 %reduce-scatter.24.cloned.1.call-done = bf16[256,1,1024]{2,0,1:T(8,128)(2,1)} async-done(((bf16[2048,1,1024]{2,0,1:T(8,128)(2,1)}), bf16[256,1,1024]{2,0,1:T(8,128)(2,1)}) %reduce-scatter.24.cloned.1.call-update) | async-done | bytes 524304 | tf_op jit(solution)/shard_map/reduce_scatter | solution.py:161
  576.4 72.5 %all-gather.17.cloned.1.call-done = bf16[2048,1,1024]{2,0,1:T(8,128)(2,1)} async-done(((bf16[256,1,1024]{2,0,1:T(8,128)(2,1)}), bf16[2048,1,1024]{2,0,1:T(8,128)(2,1)}) %all-gather.17.cloned.1.call-update) | async-done | bytes 4194320 | tf_op jit(solution)/shard_map/all_gather | solution.py:183
  649.0 7.0 convert_reduce_fusion.1
  662.1 86.5 %reduce-scatter.30.cloned.1.call-done = bf16[256,1,1024]{2,0,1:T(8,128)(2,1)} async-done(((bf16[2048,1,1024]{2,0,1:T(8,128)(2,1)}), bf16[256,1,1024]{2,0,1:T(8,128)(2,1)}) %reduce-scatter.30.cloned.1.call-update) | async-done | bytes 524304 | tf_op jit(solution)/shard_map/reduce_scatter | solution.py:195
  753.1 72.5 %all-gather.15.cloned.1.call-done = bf16[2048,1,1024]{2,0,1:T(8,128)(2,1)} async-done(((bf16[256,1,1024]{2,0,1:T(8,128)(2,1)}), bf16[2048,1,1024]{2,0,1:T(8,128)(2,1)}) %all-gather.15.cloned.1.call-update) | async-done | bytes 4194320 | tf_op jit(solution)/shard_map/all_gather | solution.py:155
  825.7 13.9 fusion.9
  845.9 86.3 %reduce-scatter.28.cloned.1.call-done = bf16[256,1,1024]{2,0,1:T(8,128)(2,1)} async-done(((bf16[2048,1,1024]{2,0,1:T(8,128)(2,1)}), bf16[256,1,1024]{2,0,1:T(8,128)(2,1)}) %reduce-scatter.28.cloned.1.call-update) | async-done | bytes 524304 | tf_op jit(solution)/shard_map/reduce_scatter | solution.py:161
  944.5 67.8 %all-gather.21.cloned.1.call-done = bf16[2048,1,1024]{2,0,1:T(8,128)(2,1)} async-done(((bf16[256,1,1024]{2,0,1:T(8,128)(2,1)}), bf16[2048,1,1024]{2,0,1:T(8,128)(2,1)}) %all-gather.21.cloned.1.call-update) | async-done | bytes 4194320 | tf_op jit(solution)/shard_map/all_gather | solution.py:183
  1012.3 7.0 convert_reduce_fusion
  1025.2 60.4 %all-gather.19.cloned.1.call-done = bf16[2048,1,1024]{2,0,1:T(8,128)(2,1)} async-done(((bf16[256,1,1024]{2,0,1:T(8,128)(2,1)}), bf16[2048,1,1024]{2,0,1:T(8,128)(2,1)}) %all-gather.19.cloned.1.call-update) | async-done | bytes 4194320 | tf_op jit(solution)/shard_map/all_gather | solution.py:208
  1096.6 79.5 %reduce-scatter.34.cloned.1.call-done = bf16[256,1,1024]{2,0,1:T(8,128)(2,1)} async-done(((bf16[2048,1,1024]{2,0,1:T(8,128)(2,1)}), bf16[256,1,1024]{2,0,1:T(8,128)(2,1)}) %reduce-scatter.34.cloned.1.call-update) | async-done | bytes 524304 | tf_op jit(solution)/shard_map/reduce_scatter | solution.py:195
  1183.1 7.1 multiply_convert_fusion.3
  1192.5 14.9 multiply_reduce_fusion.1
  1207.5 8.0 multiply_convert_fusion.1
  1234.1 8.0 convert_reduce_fusion.4
  1289.5 8.0 multiply_reduce_fusion
  1297.5 8.1 multiply_convert_fusion
  1309.2 8.7 convert_reduce_fusion.2
  1347.8 20.1 %reduce-scatter.48.cloned.1.call-done = bf16[128,1]{1,0:T(8,128)(2,1)} async-done(((bf16[512,1]{1,0:T(8,128)(2,1)}), bf16[128,1]{1,0:T(8,128)(2,1)}) %reduce-scatter.48.cloned.1.call-update) | async-done | bytes 272
  1369.3 25.8 %reduce-scatter.44.cloned.1.call-done = bf16[512,256]{1,0:T(8,128)(2,1)} async-done(((bf16[512,1024]{1,0:T(8,128)(2,1)}), bf16[512,256]{1,0:T(8,128)(2,1)}) %reduce-scatter.44.cloned.1.call-update) | async-done | bytes 262160 | tf_op jit(solution)/shard_map/reduce_scatter | solution.py:301
  1396.9 26.0 %reduce-scatter.42.cloned.1.call-done = bf16[1,256,512]{2,1,0:T(8,128)(2,1)} async-done(((bf16[1,1024,512]{2,1,0:T(8,128)(2,1)}), bf16[1,256,512]{2,1,0:T(8,128)(2,1)}) %reduce-scatter.42.cloned.1.call-update) | async-done | bytes 262160 | tf_op jit(solution)/shard_map/reduce_scatter | solution.py:301
  1424.7 136.4 %reduce-scatter.50.cloned.1.call-done = f32[32,6]{1,0:T(8,128)} async-done(((f32[1024,6]{1,0:T(8,128)}), f32[32,6]{1,0:T(8,128)}) %reduce-scatter.50.cloned.1.call-update) | async-done | bytes 784
  1562.4 16.8 reduce-scatter.46.cloned.1.call-done
  1580.5 21.8 %reduce-scatter.40.cloned.1.call-done = bf16[128,256]{1,0:T(8,128)(2,1)} async-done(((bf16[128,1024]{1,0:T(8,128)(2,1)}), bf16[128,256]{1,0:T(8,128)(2,1)}) %reduce-scatter.40.cloned.1.call-update) | async-done | bytes 65552 | tf_op jit(solution)/shard_map/reduce_scatter | solution.py:301
  1603.8 24.3 %reduce-scatter.38.cloned.1.call-done = bf16[3,256,128]{1,2,0:T(8,128)(2,1)} async-done(((bf16[3,1024,128]{1,2,0:T(8,128)(2,1)}), bf16[3,256,128]{1,2,0:T(8,128)(2,1)}) %reduce-scatter.38.cloned.1.call-update) | async-done | bytes 196624 | tf_op jit(solution)/shard_map/reduce_scatter | solution.py:301
  1629.9 90.2 %reduce-scatter.36.cloned.1.call-done = bf16[256,1,1024]{2,0,1:T(8,128)(2,1)} async-done(((bf16[2048,1,1024]{2,0,1:T(8,128)(2,1)}), bf16[256,1,1024]{2,0,1:T(8,128)(2,1)}) %reduce-scatter.36.cloned.1.call-update) | async-done | bytes 524304 | tf_op jit(solution)/shard_map/reduce_scatter | solution.py:277
  (474 shorter events, 255.9 us)
Async XLA Ops:
  7.2 454.5 %copy-start = (bf16[1024,512]{1,0:T(8,128)(2,1)S(1)}, bf16[1024,512]{1,0:T(8,128)(2,1)}, u32[]{:S(2)}) copy-start(bf16[1024,512]{1,0:T(8,128)(2,1)} %param.28) | copy-start | bytes 3145732
  7.2 79.1 %all-gather.9.cloned.1.call-start = ((), (), s32[]{:S(2)}) async-start(), calls=%async_computation.15 | async-start | bytes 4718592 | tf_op jit(solution)/shard_map/all_gather | solution.py:98
  8.2 189.6 %copy-start.82 = (f32[1,1,1024]{2,1,0:T(1,128)}, f32[1,1,1024]{2,1,0:T(1,128)S(1)}, u32[]{:S(2)}) copy-start(f32[1,1,1024]{2,1,0:T(1,128)S(1)} %get-tuple-element.128) | copy-start | bytes 12292
  10.6 187.3 %reduce-scatter.22.cloned.1.call-start = ((), (), s32[]{:S(2)}) async-start(), calls=%async_computation.16 | async-start | bytes 4718592 | tf_op jit(solution)/shard_map/reduce_scatter | solution.py:143
  106.5 91.4 %copy-start.8 = (bf16[2,256,1,1024]{3,1,2,0:T(8,128)(2,1)S(1)}, bf16[2,256,1,1024]{3,1,2,0:T(8,128)(2,1)}, u32[]{:S(2)}) copy-start(bf16[2,256,1,1024]{3,1,2,0:T(8,128)(2,1)} %param.17) | copy-start | bytes 3145732
  110.9 162.5 %copy-start.65 = (bf16[3,1024,128]{1,2,0:T(8,128)(2,1)S(1)}, bf16[3,1024,128]{1,2,0:T(8,128)(2,1)}, u32[]{:S(2)}) copy-start(bf16[3,1024,128]{1,2,0:T(8,128)(2,1)} %copy-done.64) | copy-start | bytes 2359300
  110.9 162.4 %all-gather.13.cloned.1.call-start = ((), (), s32[]{:S(2)}) async-start(), calls=%async_computation.19 | async-start | bytes 4718592 | tf_op jit(solution)/shard_map/all_gather | solution.py:98
  200.8 185.3 %reduce-scatter.26.cloned.1.call-start = ((), (), s32[]{:S(2)}) async-start(), calls=%async_computation.20 | async-start | bytes 4718592 | tf_op jit(solution)/shard_map/reduce_scatter | solution.py:143
  294.6 91.4 %copy-start.10 = (bf16[256,1,1024]{2,0,1:T(8,128)(2,1)S(1)}, bf16[256,1,1024]{2,0,1:T(8,128)(2,1)}, u32[]{:S(2)}) copy-start(bf16[256,1,1024]{2,0,1:T(8,128)(2,1)} %reduce-scatter.22.cloned.1.call-done) | copy-start | bytes 1572868
  294.6 91.4 %copy-start.83 = (f32[1,1,1024]{2,1,0:T(1,128)S(1)}, f32[1,1,1024]{2,1,0:T(1,128)}, u32[]{:S(2)}) copy-start(f32[1,1,1024]{2,1,0:T(1,128)} %copy-done.82) | copy-start | bytes 12292
  294.6 91.4 %copy-start.89 = (pred[256]{0:T(512)(128)(4,1)S(1)}, pred[256]{0:T(512)(128)(4,1)}, u32[]{:S(2)}) copy-start(pred[256]{0:T(512)(128)(4,1)} %copy-done.87) | copy-start | bytes 772
  299.0 162.7 %copy-start.119 = (f32[512]{0:T(512)S(1)}, f32[512]{0:T(512)}, u32[]{:S(2)}) copy-start(f32[512]{0:T(512)} %param.29) | copy-start | bytes 6148
  299.0 162.6 %all-gather.11.cloned.1.call-start = ((), (), s32[]{:S(2)}) async-start(), calls=%async_computation.17 | async-start | bytes 4718592 | tf_op jit(solution)/shard_map/all_gather | solution.py:155
  389.1 179.4 %reduce-scatter.24.cloned.1.call-start = ((), (), s32[]{:S(2)}) async-start(), calls=%async_computation.18 | async-start | bytes 4718592 | tf_op jit(solution)/shard_map/reduce_scatter | solution.py:161
  481.5 167.5 %all-gather.17.cloned.1.call-start = ((), (), s32[]{:S(2)}) async-start(), calls=%async_computation.23 | async-start | bytes 4718592 | tf_op jit(solution)/shard_map/all_gather | solution.py:183
  576.4 172.2 %reduce-scatter.30.cloned.1.call-start = ((), (), s32[]{:S(2)}) async-start(), calls=%async_computation.24 | async-start | bytes 4718592 | tf_op jit(solution)/shard_map/reduce_scatter | solution.py:195
  661.6 164.0 %all-gather.15.cloned.1.call-start = ((), (), s32[]{:S(2)}) async-start(), calls=%async_computation.21 | async-start | bytes 4718592 | tf_op jit(solution)/shard_map/all_gather | solution.py:155
  753.1 179.1 %reduce-scatter.28.cloned.1.call-start = ((), (), s32[]{:S(2)}) async-start(), calls=%async_computation.22 | async-start | bytes 4718592 | tf_op jit(solution)/shard_map/reduce_scatter | solution.py:161
  845.2 167.1 %all-gather.21.cloned.1.call-start = ((), (), s32[]{:S(2)}) async-start(), calls=%async_computation.27 | async-start | bytes 4718592 | tf_op jit(solution)/shard_map/all_gather | solution.py:183
  939.7 145.9 %all-gather.19.cloned.1.call-start = ((), (), s32[]{:S(2)}) async-start(), calls=%async_computation.25 | async-start | bytes 4718592 | tf_op jit(solution)/shard_map/all_gather | solution.py:208
  944.2 231.9 %reduce-scatter.34.cloned.1.call-start = ((), (), s32[]{:S(2)}) async-start(), calls=%async_computation.28 | async-start | bytes 4718592 | tf_op jit(solution)/shard_map/reduce_scatter | solution.py:195
  1025.1 241.8 %all-gather.23.cloned.1.call-start = ((), (), s32[]{:S(2)}) async-start(), calls=%async_computation.29 | async-start | bytes 4718592 | tf_op jit(solution)/shard_map/all_gather | solution.py:208
  1182.8 163.8 %reduce-scatter.32.cloned.1.call-start = ((), (), s32[]{:S(2)}) async-start(), calls=%async_computation.26 | async-start | bytes 4718592 | tf_op jit(solution)/shard_map/reduce_scatter | solution.py:277
  1246.9 121.0 %reduce-scatter.48.cloned.1.call-start = ((), (), s32[]{:S(2)}) async-start(), calls=%async_computation.36 | async-start | bytes 163840
  1248.4 146.7 %reduce-scatter.44.cloned.1.call-start = ((), (), s32[]{:S(2)}) async-start(), calls=%async_computation.34 | async-start | bytes 1310720 | tf_op jit(solution)/shard_map/reduce_scatter | solution.py:301
  1256.6 166.3 %reduce-scatter.42.cloned.1.call-start = ((), (), s32[]{:S(2)}) async-start(), calls=%async_computation.33 | async-start | bytes 1310720 | tf_op jit(solution)/shard_map/reduce_scatter | solution.py:301
  1264.9 296.2 %reduce-scatter.50.cloned.1.call-start = ((), (), s32[]{:S(2)}) async-start(), calls=%async_computation.37 | async-start | bytes 540672
  1266.9 312.3 %reduce-scatter.46.cloned.1.call-start = ((), (), s32[]{:S(2)}) async-start(), calls=%async_computation.35 | async-start | bytes 40960
  1323.8 278.5 %reduce-scatter.40.cloned.1.call-start = ((), (), s32[]{:S(2)}) async-start(), calls=%async_computation.32 | async-start | bytes 327680 | tf_op jit(solution)/shard_map/reduce_scatter | solution.py:301
  1330.8 297.2 %reduce-scatter.38.cloned.1.call-start = ((), (), s32[]{:S(2)}) async-start(), calls=%async_computation.31 | async-start | bytes 983040 | tf_op jit(solution)/shard_map/reduce_scatter | solution.py:301
  1338.7 381.4 %reduce-scatter.36.cloned.1.call-start = ((), (), s32[]{:S(2)}) async-start(), calls=%async_computation.30 | async-start | bytes 4718592 | tf_op jit(solution)/shard_map/reduce_scatter | solution.py:277
  1344.4 375.7 %copy-start.19 = (f32[256,1,1024]{2,0,1:T(8,128)S(1)}, f32[256,1,1024]{2,0,1:T(8,128)}, u32[]{:S(2)}) copy-start(f32[256,1,1024]{2,0,1:T(8,128)} %copy-done.18) | copy-start | bytes 3145732
  (128 other events, 1864.8 us)
Sparse Core Ops, SparseCore 0:
  10.7 75.5 all-gather.8
  111.0 86.8 reduce-scatter.21
  200.9 72.4 all-gather.12
  299.2 86.8 reduce-scatter.25
  389.2 72.4 all-gather.10
  481.6 86.8 reduce-scatter.23
  576.5 72.4 all-gather.16
  661.8 86.8 reduce-scatter.29
  753.2 72.4 all-gather.14
  845.3 86.8 reduce-scatter.27
  939.8 72.4 all-gather.20
  1014.3 71.3 all-gather.18
  1089.2 86.8 reduce-scatter.33
  1182.9 72.4 all-gather.22
  1258.9 86.8 reduce-scatter.31
  1348.6 19.2 reduce-scatter.47
  1370.3 24.7 reduce-scatter.43
  1398.0 24.7 reduce-scatter.41
  1425.1 135.8 reduce-scatter.49
  1563.3 15.8 reduce-scatter.45
  1582.2 20.0 reduce-scatter.39
  1604.8 23.1 reduce-scatter.37
  1631.7 88.3 reduce-scatter.35
where the time goes:
time: 1740 us; the launch traced here: 1730 us
  waiting for transfers between devices  1360 us (78%)
  matrix products  224 us (13%)
  other arithmetic  89 us (5%)
  local copies, waits for them, and re-layouts  39.1 us (2%)
    reduce_scatter x2, waiting for transfers between devices, body(): lax.psum_scatter(jnp.einsum('sic,cd->sid', context, out_weight, preferred...  174 us
    unnamed x26, waiting for transfers between devices  174 us
    reduce_scatter x2, waiting for transfers between devices, body(): lax.psum_scatter(jnp.einsum('sif,df->sid', grad_pre, up_weight, preferred...  166 us
    reduce_scatter x2, waiting for transfers between devices, body(): lax.psum_scatter(jnp.einsum('sif,fd->sid', act_low, down_weight, preferre...  163 us
    all_gather x2, waiting for transfers between devices, body(): normed_all = lax.all_gather(normed_low, 'tensor', axis=0, tiled=True)  145 us
    all_gather x2, waiting for transfers between devices, body(): hidden_all = lax.all_gather(hidden_low, 'tensor', axis=0, tiled=True)  145 us
    all_gather x2, waiting for transfers between devices, body(): lax.all_gather(grad_sum.astype(jnp.bfloat16), 'tensor', axis=0, tiled=True)  140 us
    reduce_scatter x4, waiting for transfers between devices, body(): lax.psum_scatter(as_sent(totals), 'dp', scatter_dimension=1, tiled=True)  97.9 us
  transfers between devices with their start and end apart: 23, of which 21 were waited for; matrix products, arithmetic and copies ran while one was open for 11% of the time, Pallas kernels for 0%

commit v1 on v0

--- a/solution.py
+++ b/solution.py
@@ -95,7 +95,15 @@
         temb = jnp.where(late[:, None, None], embedded[None, :, 1], embedded[None, :, 0])
         hidden = tokens[index].astype(jnp.float32) + temb
         hidden_low = hidden.astype(jnp.bfloat16)
-        hidden_all = lax.all_gather(hidden_low, "tensor", axis=0, tiled=True)
+        ways, here = (lax.axis_size("tensor"), lax.axis_index("tensor"))
+        grown, reach = (hidden_low, 1)
+        while reach < ways:
+            theirs = lax.ppermute(grown, "tensor", [(d, d ^ reach) for d in range(ways)])
+            mine_first = jnp.concatenate([grown, theirs], axis=0)
+            theirs_first = jnp.concatenate([theirs, grown], axis=0)
+            grown = jnp.where(here & reach == 0, mine_first, theirs_first)
+            reach = 2 * reach
+        hidden_all = grown
         projected = jnp.einsum(
             "sid,kdc->ksic", hidden_all, qkv_weight, preferred_element_type=jnp.float32
         )

time: 1740 us -> 1860 us (1.069)
  waiting for transfers between devices: 1360 us -> 1450 us
    ppermute x0 -> x6, waiting for transfers between devices: none -> 237 us  [body(): lax.ppermute(grown, 'tensor', [(d, d ^ reach) for d in range(ways)])]
    all_gather x2 -> x0, waiting for transfers between devices: 145 us -> none  [body(): hidden_all = lax.all_gather(hidden_low, 'tensor', axis=0, tiled=True)]
    unnamed x26 -> x24, waiting for transfers between devices: 174 us -> 168 us
  transfers between devices with their start and end apart: 23 -> 27, of which waited for: 21 -> 25; matrix products, arithmetic and copies ran while one was open for 11% -> 11% of each run, Pallas kernels for 0% -> 0%
where the time goes in v1:
time: 1860 us
  waiting for transfers between devices  1450 us (78%)
  matrix products  230 us (12%)
  other arithmetic  103 us (6%)
  local copies, waits for them, and re-layouts  38.8 us (2%)
    ppermute x6, waiting for transfers between devices, body(): lax.ppermute(grown, 'tensor', [(d, d ^ reach) for d in range(ways)])  237 us
    reduce_scatter x2, waiting for transfers between devices, body(): lax.psum_scatter(jnp.einsum('sic,cd->sid', context, out_weight, preferred...  179 us
    unnamed x24, waiting for transfers between devices  168 us
    reduce_scatter x2, waiting for transfers between devices, body(): lax.psum_scatter(jnp.einsum('sif,df->sid', grad_pre, up_weight, preferred...  166 us
    reduce_scatter x2, waiting for transfers between devices, body(): lax.psum_scatter(jnp.einsum('sif,fd->sid', act_low, down_weight, preferre...  163 us
    all_gather x2, waiting for transfers between devices, body(): normed_all = lax.all_gather(normed_low, 'tensor', axis=0, tiled=True)  145 us
    all_gather x2, waiting for transfers between devices, body(): lax.all_gather(grad_sum.astype(jnp.bfloat16), 'tensor', axis=0, tiled=True)  140 us
    reduce_scatter x4, waiting for transfers between devices, body(): lax.psum_scatter(as_sent(totals), 'dp', scatter_dimension=1, tiled=True)  97.8 us
  transfers between devices with their start and end apart: 27, of which 25 were waited for; matrix products, arithmetic and copies ran while one was open for 11% of the time, Pallas kernels for 0%

profile of v1, /device:TPU:0, one launch (start us, length us, event | category | flops | bytes accessed | tf_op | source)
XLA Modules:
  0.0 1857.4 jit_solution(12006497996320003688)
XLA Ops:
  14.1 10.4 collective-permute-done
  29.4 21.2 %collective-permute-done.1 = bf16[512,1,1024]{2,0,1:T(8,128)(2,1)} collective-permute-done((bf16[512,1,1024]{2,0,1:T(8,128)(2,1)}, bf16[512,1,1024]{2,0,1:T(8,128)(2,1)}, u32[]{:S(2)}, u32[]{:S(2)}) %collective-permute-start.1) | collective-permute-done | bytes 1048608 | tf_op jit(solution)/shard_map/ppermute | solution.py:101
  62.3 84.3 %collective-permute-done.2 = bf16[1024,1,1024]{2,0,1:T(8,128)(2,1)} collective-permute-done((bf16[1024,1,1024]{2,0,1:T(8,128)(2,1)}, bf16[1024,1,1024]{2,0,1:T(8,128)(2,1)}, u32[]{:S(2)}, u32[]{:S(2)}) %collective-permute-start.2) | collective-permute-done | bytes 2097184 | tf_op jit(solution)/shard_map/ppermute | solution.py:101
  176.7 89.2 %reduce-scatter.22.cloned.1.call-done = bf16[256,1,1024]{2,0,1:T(8,128)(2,1)} async-done(((bf16[2048,1,1024]{2,0,1:T(8,128)(2,1)}), bf16[256,1,1024]{2,0,1:T(8,128)(2,1)}) %reduce-scatter.22.cloned.1.call-update) | async-done | bytes 524304 | tf_op jit(solution)/shard_map/reduce_scatter | solution.py:151
  269.5 11.8 collective-permute-done.3
  284.0 21.5 %collective-permute-done.4 = bf16[512,1,1024]{2,0,1:T(8,128)(2,1)S(1)} collective-permute-done((bf16[512,1,1024]{2,0,1:T(8,128)(2,1)S(1)}, bf16[512,1,1024]{2,0,1:T(8,128)(2,1)S(1)}, u32[]{:S(2)}, u32[]{:S(2)}) %collective-permute-start.4) | collective-permute-done | bytes 1048608 | tf_op jit(solution)/shard_map/ppermute | solution.py:101
  310.3 87.8 %collective-permute-done.5 = bf16[1024,1,1024]{2,0,1:T(8,128)(2,1)S(1)} collective-permute-done((bf16[1024,1,1024]{2,0,1:T(8,128)(2,1)S(1)}, bf16[1024,1,1024]{2,0,1:T(8,128)(2,1)S(1)}, u32[]{:S(2)}, u32[]{:S(2)}) %collective-permute-start.5) | collective-permute-done | bytes 2097184 | tf_op jit(solution)/shard_map/ppermute | solution.py:101
  421.8 89.4 %reduce-scatter.26.cloned.1.call-done = bf16[256,1,1024]{2,0,1:T(8,128)(2,1)} async-done(((bf16[2048,1,1024]{2,0,1:T(8,128)(2,1)}), bf16[256,1,1024]{2,0,1:T(8,128)(2,1)}) %reduce-scatter.26.cloned.1.call-update) | async-done | bytes 524304 | tf_op jit(solution)/shard_map/reduce_scatter | solution.py:151
  514.3 72.5 %all-gather.7.cloned.1.call-done = bf16[2048,1,1024]{2,0,1:T(8,128)(2,1)} async-done(((bf16[256,1,1024]{2,0,1:T(8,128)(2,1)}), bf16[2048,1,1024]{2,0,1:T(8,128)(2,1)}) %all-gather.7.cloned.1.call-update) | async-done | bytes 4194320 | tf_op jit(solution)/shard_map/all_gather | solution.py:163
  586.8 14.2 fusion.6
  616.8 77.0 %reduce-scatter.24.cloned.1.call-done = bf16[256,1,1024]{2,0,1:T(8,128)(2,1)} async-done(((bf16[2048,1,1024]{2,0,1:T(8,128)(2,1)}), bf16[256,1,1024]{2,0,1:T(8,128)(2,1)}) %reduce-scatter.24.cloned.1.call-update) | async-done | bytes 524304 | tf_op jit(solution)/shard_map/reduce_scatter | solution.py:169
  701.8 72.5 %all-gather.11.cloned.1.call-done = bf16[2048,1,1024]{2,0,1:T(8,128)(2,1)} async-done(((bf16[256,1,1024]{2,0,1:T(8,128)(2,1)}), bf16[2048,1,1024]{2,0,1:T(8,128)(2,1)}) %all-gather.11.cloned.1.call-update) | async-done | bytes 4194320 | tf_op jit(solution)/shard_map/all_gather | solution.py:191
  787.2 86.8 %reduce-scatter.30.cloned.1.call-done = bf16[256,1,1024]{2,0,1:T(8,128)(2,1)} async-done(((bf16[2048,1,1024]{2,0,1:T(8,128)(2,1)}), bf16[256,1,1024]{2,0,1:T(8,128)(2,1)}) %reduce-scatter.30.cloned.1.call-update) | async-done | bytes 524304 | tf_op jit(solution)/shard_map/reduce_scatter | solution.py:203
  878.4 72.5 %all-gather.9.cloned.1.call-done = bf16[2048,1,1024]{2,0,1:T(8,128)(2,1)} async-done(((bf16[256,1,1024]{2,0,1:T(8,128)(2,1)}), bf16[2048,1,1024]{2,0,1:T(8,128)(2,1)}) %all-gather.9.cloned.1.call-update) | async-done | bytes 4194320 | tf_op jit(solution)/shard_map/all_gather | solution.py:163
  951.0 13.8 fusion.9
  971.1 86.3 %reduce-scatter.28.cloned.1.call-done = bf16[256,1,1024]{2,0,1:T(8,128)(2,1)} async-done(((bf16[2048,1,1024]{2,0,1:T(8,128)(2,1)}), bf16[256,1,1024]{2,0,1:T(8,128)(2,1)}) %reduce-scatter.28.cloned.1.call-update) | async-done | bytes 524304 | tf_op jit(solution)/shard_map/reduce_scatter | solution.py:169
  1069.7 67.8 %all-gather.15.cloned.1.call-done = bf16[2048,1,1024]{2,0,1:T(8,128)(2,1)} async-done(((bf16[256,1,1024]{2,0,1:T(8,128)(2,1)}), bf16[2048,1,1024]{2,0,1:T(8,128)(2,1)}) %all-gather.15.cloned.1.call-update) | async-done | bytes 4194320 | tf_op jit(solution)/shard_map/all_gather | solution.py:191
  1150.3 60.6 %all-gather.13.cloned.1.call-done = bf16[2048,1,1024]{2,0,1:T(8,128)(2,1)} async-done(((bf16[256,1,1024]{2,0,1:T(8,128)(2,1)}), bf16[2048,1,1024]{2,0,1:T(8,128)(2,1)}) %all-gather.13.cloned.1.call-update) | async-done | bytes 4194320 | tf_op jit(solution)/shard_map/all_gather | solution.py:216
  1221.9 79.5 %reduce-scatter.34.cloned.1.call-done = bf16[256,1,1024]{2,0,1:T(8,128)(2,1)} async-done(((bf16[2048,1,1024]{2,0,1:T(8,128)(2,1)}), bf16[256,1,1024]{2,0,1:T(8,128)(2,1)}) %reduce-scatter.34.cloned.1.call-update) | async-done | bytes 524304 | tf_op jit(solution)/shard_map/reduce_scatter | solution.py:203
  1317.9 15.2 multiply_reduce_fusion.1
  1360.3 8.4 convert_reduce_fusion.4
  1416.6 8.0 multiply_reduce_fusion
  1424.6 8.1 multiply_convert_fusion
  1436.3 8.6 convert_reduce_fusion.2
  1478.5 14.8 reduce-scatter.48.cloned.1.call-done
  1494.6 25.8 %reduce-scatter.44.cloned.1.call-done = bf16[512,256]{1,0:T(8,128)(2,1)} async-done(((bf16[512,1024]{1,0:T(8,128)(2,1)}), bf16[512,256]{1,0:T(8,128)(2,1)}) %reduce-scatter.44.cloned.1.call-update) | async-done | bytes 262160 | tf_op jit(solution)/shard_map/reduce_scatter | solution.py:309
  1522.2 25.4 %reduce-scatter.42.cloned.1.call-done = bf16[1,256,512]{2,1,0:T(8,128)(2,1)} async-done(((bf16[1,1024,512]{2,1,0:T(8,128)(2,1)}), bf16[1,256,512]{2,1,0:T(8,128)(2,1)}) %reduce-scatter.42.cloned.1.call-update) | async-done | bytes 262160 | tf_op jit(solution)/shard_map/reduce_scatter | solution.py:309
  1549.5 136.1 %reduce-scatter.50.cloned.1.call-done = f32[32,6]{1,0:T(8,128)} async-done(((f32[1024,6]{1,0:T(8,128)}), f32[32,6]{1,0:T(8,128)}) %reduce-scatter.50.cloned.1.call-update) | async-done | bytes 784
  1687.0 16.8 reduce-scatter.46.cloned.1.call-done
  1705.1 21.8 %reduce-scatter.40.cloned.1.call-done = bf16[128,256]{1,0:T(8,128)(2,1)} async-done(((bf16[128,1024]{1,0:T(8,128)(2,1)}), bf16[128,256]{1,0:T(8,128)(2,1)}) %reduce-scatter.40.cloned.1.call-update) | async-done | bytes 65552 | tf_op jit(solution)/shard_map/reduce_scatter | solution.py:309
  1728.4 24.7 %reduce-scatter.38.cloned.1.call-done = bf16[3,256,128]{1,2,0:T(8,128)(2,1)} async-done(((bf16[3,1024,128]{1,2,0:T(8,128)(2,1)}), bf16[3,256,128]{1,2,0:T(8,128)(2,1)}) %reduce-scatter.38.cloned.1.call-update) | async-done | bytes 196624 | tf_op jit(solution)/shard_map/reduce_scatter | solution.py:309
  1754.9 90.2 %reduce-scatter.36.cloned.1.call-done = bf16[256,1,1024]{2,0,1:T(8,128)(2,1)} async-done(((bf16[2048,1,1024]{2,0,1:T(8,128)(2,1)}), bf16[256,1,1024]{2,0,1:T(8,128)(2,1)}) %reduce-scatter.36.cloned.1.call-update) | async-done | bytes 524304 | tf_op jit(solution)/shard_map/reduce_scatter | solution.py:285
  (501 shorter events, 317.4 us)
Async XLA Ops:
  7.2 579.6 %copy-start = (bf16[1024,512]{1,0:T(8,128)(2,1)S(1)}, bf16[1024,512]{1,0:T(8,128)(2,1)}, u32[]{:S(2)}) copy-start(bf16[1024,512]{1,0:T(8,128)(2,1)} %param.28) | copy-start | bytes 3145732
  7.2 258.7 %reduce-scatter.22.cloned.1.call-start = ((), (), s32[]{:S(2)}) async-start(), calls=%async_computation.15 | async-start | bytes 4718592 | tf_op jit(solution)/shard_map/reduce_scatter | solution.py:151
  8.2 257.7 %copy-start.80 = (f32[1,1,1024]{2,1,0:T(1,128)}, f32[1,1,1024]{2,1,0:T(1,128)S(1)}, u32[]{:S(2)}) copy-start(f32[1,1,1024]{2,1,0:T(1,128)S(1)} %get-tuple-element.130) | copy-start | bytes 12292
  9.5 15.0 collective-permute-start
  26.0 24.6 %collective-permute-start.1 = (bf16[512,1,1024]{2,0,1:T(8,128)(2,1)}, bf16[512,1,1024]{2,0,1:T(8,128)(2,1)}, u32[]{:S(2)}, u32[]{:S(2)}) collective-permute-start(bf16[512,1,1024]{2,0,1:T(8,128)(2,1)} %maximum_select_fusion.7), channel_id=1, source_target_pairs={{0,2},{1,3},{2,0},{3,1},{4,6},{5,7},{6,4},{7,5},{8,10},{9,11},{10,... | collective-permute-start | bytes 3145736 | tf_op jit(solution)/shard_map/ppermute | solution.py:101
  54.5 92.1 %collective-permute-start.2 = (bf16[1024,1,1024]{2,0,1:T(8,128)(2,1)}, bf16[1024,1,1024]{2,0,1:T(8,128)(2,1)}, u32[]{:S(2)}, u32[]{:S(2)}) collective-permute-start(bf16[1024,1,1024]{2,0,1:T(8,128)(2,1)} %maximum_select_fusion.3), channel_id=1, source_target_pairs={{0,4},{1,5},{2,6},{3,7},{4,0},{5,1},{6,2},{7,3},{8,12},{9,13},{10,... | collective-permute-start | bytes 6291464 | tf_op jit(solution)/shard_map/ppermute | solution.py:101
  58.5 95.6 %copy-start.66 = (bf16[3,1024,128]{1,2,0:T(8,128)(2,1)}, bf16[3,1024,128]{1,2,0:T(8,128)(2,1)S(1)}, u32[]{:S(2)}) copy-start(bf16[3,1024,128]{1,2,0:T(8,128)(2,1)S(1)} %copy.47) | copy-start | bytes 2359300
  176.6 334.6 %reduce-scatter.26.cloned.1.call-start = ((), (), s32[]{:S(2)}) async-start(), calls=%async_computation.18 | async-start | bytes 4718592 | tf_op jit(solution)/shard_map/reduce_scatter | solution.py:151
  268.0 13.3 collective-permute-start.3
  281.8 23.7 %collective-permute-start.4 = (bf16[512,1,1024]{2,0,1:T(8,128)(2,1)S(1)}, bf16[512,1,1024]{2,0,1:T(8,128)(2,1)S(1)}, u32[]{:S(2)}, u32[]{:S(2)}) collective-permute-start(bf16[512,1,1024]{2,0,1:T(8,128)(2,1)S(1)} %maximum_select_fusion.9), channel_id=1, source_target_pairs={{0,2},{1,3},{2,0},{3,1},{4,6},{5,7},{6,4},{7,5},{8,10},{9,11},{10,... | collective-permute-start | bytes 3145736 | tf_op jit(solution)/shard_map/ppermute | solution.py:101
  306.5 91.6 %collective-permute-start.5 = (bf16[1024,1,1024]{2,0,1:T(8,128)(2,1)S(1)}, bf16[1024,1,1024]{2,0,1:T(8,128)(2,1)S(1)}, u32[]{:S(2)}, u32[]{:S(2)}) collective-permute-start(bf16[1024,1,1024]{2,0,1:T(8,128)(2,1)S(1)} %maximum_select_fusion.5), channel_id=1, source_target_pairs={{0,4},{1,5},{2,6},{3,7},{4,0},{5,1},{6,2},{7,3},{8,12},{9,13},{10,... | collective-permute-start | bytes 6291464 | tf_op jit(solution)/shard_map/ppermute | solution.py:101
  421.7 165.1 %copy-start.125 = (f32[512]{0:T(512)S(1)}, f32[512]{0:T(512)}, u32[]{:S(2)}) copy-start(f32[512]{0:T(512)} %param.29) | copy-start | bytes 6148
  421.7 165.1 %all-gather.7.cloned.1.call-start = ((), (), s32[]{:S(2)}) async-start(), calls=%async_computation.16 | async-start | bytes 4718592 | tf_op jit(solution)/shard_map/all_gather | solution.py:163
  514.2 179.6 %reduce-scatter.24.cloned.1.call-start = ((), (), s32[]{:S(2)}) async-start(), calls=%async_computation.17 | async-start | bytes 4718592 | tf_op jit(solution)/shard_map/reduce_scatter | solution.py:169
  606.8 167.5 %all-gather.11.cloned.1.call-start = ((), (), s32[]{:S(2)}) async-start(), calls=%async_computation.21 | async-start | bytes 4718592 | tf_op jit(solution)/shard_map/all_gather | solution.py:191
  701.7 172.2 %reduce-scatter.30.cloned.1.call-start = ((), (), s32[]{:S(2)}) async-start(), calls=%async_computation.22 | async-start | bytes 4718592 | tf_op jit(solution)/shard_map/reduce_scatter | solution.py:203
  786.9 164.0 %all-gather.9.cloned.1.call-start = ((), (), s32[]{:S(2)}) async-start(), calls=%async_computation.19 | async-start | bytes 4718592 | tf_op jit(solution)/shard_map/all_gather | solution.py:163
  878.4 179.0 %reduce-scatter.28.cloned.1.call-start = ((), (), s32[]{:S(2)}) async-start(), calls=%async_computation.20 | async-start | bytes 4718592 | tf_op jit(solution)/shard_map/reduce_scatter | solution.py:169
  970.4 167.1 %all-gather.15.cloned.1.call-start = ((), (), s32[]{:S(2)}) async-start(), calls=%async_computation.25 | async-start | bytes 4718592 | tf_op jit(solution)/shard_map/all_gather | solution.py:191
  1065.0 145.9 %all-gather.13.cloned.1.call-start = ((), (), s32[]{:S(2)}) async-start(), calls=%async_computation.23 | async-start | bytes 4718592 | tf_op jit(solution)/shard_map/all_gather | solution.py:216
  1069.5 231.9 %reduce-scatter.34.cloned.1.call-start = ((), (), s32[]{:S(2)}) async-start(), calls=%async_computation.26 | async-start | bytes 4718592 | tf_op jit(solution)/shard_map/reduce_scatter | solution.py:203
  1150.2 243.8 %all-gather.17.cloned.1.call-start = ((), (), s32[]{:S(2)}) async-start(), calls=%async_computation.27 | async-start | bytes 4718592 | tf_op jit(solution)/shard_map/all_gather | solution.py:216
  1308.1 169.3 %reduce-scatter.32.cloned.1.call-start = ((), (), s32[]{:S(2)}) async-start(), calls=%async_computation.24 | async-start | bytes 4718592 | tf_op jit(solution)/shard_map/reduce_scatter | solution.py:285
  1373.5 119.8 %reduce-scatter.48.cloned.1.call-start = ((), (), s32[]{:S(2)}) async-start(), calls=%async_computation.34 | async-start | bytes 163840
  1375.0 145.5 %reduce-scatter.44.cloned.1.call-start = ((), (), s32[]{:S(2)}) async-start(), calls=%async_computation.32 | async-start | bytes 1310720 | tf_op jit(solution)/shard_map/reduce_scatter | solution.py:309
  1383.2 164.5 %reduce-scatter.42.cloned.1.call-start = ((), (), s32[]{:S(2)}) async-start(), calls=%async_computation.31 | async-start | bytes 1310720 | tf_op jit(solution)/shard_map/reduce_scatter | solution.py:309
  1391.5 294.1 %reduce-scatter.50.cloned.1.call-start = ((), (), s32[]{:S(2)}) async-start(), calls=%async_computation.35 | async-start | bytes 540672
  1394.0 309.7 %reduce-scatter.46.cloned.1.call-start = ((), (), s32[]{:S(2)}) async-start(), calls=%async_computation.33 | async-start | bytes 40960
  1450.9 276.0 %reduce-scatter.40.cloned.1.call-start = ((), (), s32[]{:S(2)}) async-start(), calls=%async_computation.30 | async-start | bytes 327680 | tf_op jit(solution)/shard_map/reduce_scatter | solution.py:309
  1458.3 294.8 %reduce-scatter.38.cloned.1.call-start = ((), (), s32[]{:S(2)}) async-start(), calls=%async_computation.29 | async-start | bytes 983040 | tf_op jit(solution)/shard_map/reduce_scatter | solution.py:309
  1469.2 375.9 %reduce-scatter.36.cloned.1.call-start = ((), (), s32[]{:S(2)}) async-start(), calls=%async_computation.28 | async-start | bytes 4718592 | tf_op jit(solution)/shard_map/reduce_scatter | solution.py:285
  1475.1 370.0 %copy-start.19 = (f32[256,1,1024]{2,0,1:T(8,128)S(1)}, f32[256,1,1024]{2,0,1:T(8,128)}, u32[]{:S(2)}) copy-start(f32[256,1,1024]{2,0,1:T(8,128)} %copy-done.18) | copy-start | bytes 3145732
  (138 other events, 2406.6 us)
Sparse Core Ops, SparseCore 0:
  176.7 89.1 reduce-scatter.21
  421.8 89.3 reduce-scatter.25
  514.3 72.4 all-gather.6
  606.9 86.8 reduce-scatter.23
  701.8 72.4 all-gather.10
  787.1 86.8 reduce-scatter.29
  878.5 72.4 all-gather.8
  970.6 86.8 reduce-scatter.27
  1065.1 72.4 all-gather.14
  1139.5 71.3 all-gather.12
  1214.5 86.8 reduce-scatter.33
  1308.2 72.4 all-gather.16
  1384.3 86.8 reduce-scatter.31
  1474.0 19.2 reduce-scatter.47
  1495.6 24.7 reduce-scatter.43
  1522.8 24.7 reduce-scatter.41
  1549.8 135.8 reduce-scatter.49
  1687.9 15.8 reduce-scatter.45
  1706.8 20.0 reduce-scatter.39
  1729.8 23.2 reduce-scatter.37
  1756.7 88.3 reduce-scatter.35
